TPU v7x, 32 devices: a whole 2x2x4 slice. The times are simulated.
32 devices in a mesh: gx: 8 (over z, core), gy: 4 (over y, x).
Axes of the slice: x: 2, y: 2, z: 4, core: 2. Of those that a mesh axis runs over, the one named last changes fastest.
Arguments:
- tokens: bfloat16 [64, 32, 8, 768], P('gx', 'gy'), may hold values from -64 to 64
- target: bfloat16 [64, 32, 8, 768], P('gx', 'gy'), may hold values from -4 to 4
- norm_gain: float32 [768], replicated, may hold values from 0.1 to 1.9
- qkv_weight: bfloat16 [768, 1152], P('gy'), may hold values from -4 to 4
- proj_weight: bfloat16 [384, 768], P('gy'), may hold values from -1.5 to 1.5
Outputs:
- block_out: bfloat16 [64, 32, 8, 768], P('gx', 'gy')
- qkv_grad: float32 [768, 1152], P('gy')
All inputs are finite; a program needn't handle non-finite values.
Results may differ from a plain program's by a relative error of at most 0.0094.
Values may be sent and summed in bfloat16 or wider, within the bound.
A program may use at most 64 MiB of HBM per device.

v0:
```python
import math
import jax
import jax.numpy as jnp
from jax import lax
from jax.sharding import PartitionSpec as P

HEADS = 12
HD = 32
WIN = 8
norm_eps = 1e-05


def shifted(x, axis, by):
    devices = lax.axis_size(axis)
    return lax.ppermute(x, axis, [(i, (i + by) % devices) for i in range(devices)])


def displace(volume, half_width):
    volume = jnp.roll(volume, -half_width, axis=2)
    upper_rows = shifted(volume[:half_width], "gx", -1)
    volume = jnp.concatenate([volume[half_width:], upper_rows], 0)
    upper_cols = shifted(volume[:, :half_width], "gy", -1)
    return jnp.concatenate([volume[:, half_width:], upper_cols], 1)


def restore(volume, half_width):
    lower_rows = shifted(volume[-half_width:], "gx", 1)
    volume = jnp.concatenate([lower_rows, volume[:-half_width]], 0)
    lower_cols = shifted(volume[:, -half_width:], "gy", 1)
    volume = jnp.concatenate([lower_cols, volume[:, :-half_width]], 1)
    return jnp.roll(volume, half_width, axis=2)


def into_windows(volume, window):
    ext_x, ext_y, ext_z, channels = volume.shape
    blocks = volume.reshape(ext_x, ext_y, ext_z // window, window, channels)
    return blocks.transpose(2, 0, 1, 3, 4).reshape(
        ext_z // window, ext_x * ext_y * window, channels
    )


def from_windows(windows, ext_x, ext_y, window):
    window_count = windows.shape[0]
    channels = windows.shape[2]
    blocks = windows.reshape(window_count, ext_x, ext_y, window, channels).transpose(1, 2, 0, 3, 4)
    return blocks.reshape(ext_x, ext_y, window_count * window, channels)


def head_probs(queries, keys_in, score_scale):
    scores = (
        jnp.einsum("wqd,wkd->wqk", queries, keys_in, preferred_element_type=jnp.float32)
        * score_scale
    )
    row_max = jnp.max(scores, -1, keepdims=True)
    exponent = jnp.exp(scores - row_max)
    return exponent / jnp.sum(exponent, -1, keepdims=True)


def shards(tokens, target, norm_gain, qkv_weight, proj_weight):
    window = WIN
    half_width = WIN // 2
    head_count = HEADS
    head_dim = HD
    inner_dim = HEADS * HD
    score_scale = HD ** (-0.5)
    ext_x, ext_y, ext_z, channels = tokens.shape
    total_tokens = ext_x * ext_y * ext_z * lax.axis_size("gx") * lax.axis_size("gy")
    loss_scale = 2.0 / math.sqrt(total_tokens)
    widened = tokens.astype(jnp.float32)
    token_mean = jnp.mean(widened, -1, keepdims=True)
    centred = widened - token_mean
    variance = jnp.mean(centred * centred, -1, keepdims=True)
    normed = (centred * lax.rsqrt(variance + norm_eps) * norm_gain).astype(jnp.bfloat16)
    windows_in = into_windows(displace(normed, half_width), window)
    window_count = windows_in.shape[0]
    window_tokens = windows_in.shape[1]
    flat_in = windows_in.reshape(-1, channels)
    qkv_whole = lax.all_gather(qkv_weight, "gy", axis=0, tiled=True)
    qkv_act = jnp.dot(flat_in, qkv_whole, preferred_element_type=jnp.float32).astype(jnp.bfloat16)
    qkv_act = qkv_act.reshape(window_count, window_tokens, 3 * inner_dim)

    def forward_head(head_idx, attn_buffer):
        queries = lax.dynamic_slice_in_dim(qkv_act, head_idx * head_dim, head_dim, 2)
        keys_in = lax.dynamic_slice_in_dim(qkv_act, inner_dim + head_idx * head_dim, head_dim, 2)
        values = lax.dynamic_slice_in_dim(qkv_act, 2 * inner_dim + head_idx * head_dim, head_dim, 2)
        attn_prob = head_probs(queries, keys_in, score_scale).astype(jnp.bfloat16)
        mixed = jnp.einsum(
            "wqk,wkd->wqd", attn_prob, values, preferred_element_type=jnp.float32
        ).astype(jnp.bfloat16)
        return lax.dynamic_update_slice_in_dim(attn_buffer, mixed, head_idx * head_dim, 2)

    attn_out = lax.fori_loop(
        0,
        head_count,
        forward_head,
        jnp.zeros((window_count, window_tokens, inner_dim), jnp.bfloat16),
    )
    proj_whole = lax.all_gather(proj_weight, "gy", axis=0, tiled=True)
    contract_cols = (((1,), (1,)), ((), ()))
    block_shift = jnp.dot(
        attn_out.reshape(-1, inner_dim), proj_whole, preferred_element_type=jnp.float32
    ).astype(jnp.bfloat16)
    block_shift = block_shift.reshape(window_count, window_tokens, channels)
    block_out = restore(from_windows(block_shift, ext_x, ext_y, window), half_width)
    grad_out = ((block_out.astype(jnp.float32) - target.astype(jnp.float32)) * loss_scale).astype(
        jnp.bfloat16
    )
    grad_shift = into_windows(displace(grad_out, half_width), window)
    grad_windows = lax.dot_general(
        grad_shift.reshape(-1, channels),
        proj_whole,
        contract_cols,
        preferred_element_type=jnp.float32,
    ).astype(jnp.bfloat16)
    grad_windows = grad_windows.reshape(window_count, window_tokens, inner_dim)

    def backward_head(head_idx, grad_buffer):
        queries = lax.dynamic_slice_in_dim(qkv_act, head_idx * head_dim, head_dim, 2)
        keys_in = lax.dynamic_slice_in_dim(qkv_act, inner_dim + head_idx * head_dim, head_dim, 2)
        values = lax.dynamic_slice_in_dim(qkv_act, 2 * inner_dim + head_idx * head_dim, head_dim, 2)
        attn_prob = head_probs(queries, keys_in, score_scale)
        prob_half = attn_prob.astype(jnp.bfloat16)
        grad_mixed = lax.dynamic_slice_in_dim(grad_windows, head_idx * head_dim, head_dim, 2)
        grad_probs = jnp.einsum(
            "wqd,wkd->wqk", grad_mixed, values, preferred_element_type=jnp.float32
        )
        grad_values = jnp.einsum(
            "wqk,wqd->wkd", prob_half, grad_mixed, preferred_element_type=jnp.float32
        ).astype(jnp.bfloat16)
        row_dot = jnp.sum(grad_probs * attn_prob, -1, keepdims=True)
        grad_scores = (attn_prob * (grad_probs - row_dot)).astype(jnp.bfloat16)
        grad_queries = (
            jnp.einsum("wqk,wkd->wqd", grad_scores, keys_in, preferred_element_type=jnp.float32)
            * score_scale
        ).astype(jnp.bfloat16)
        grad_keys = (
            jnp.einsum("wqk,wqd->wkd", grad_scores, queries, preferred_element_type=jnp.float32)
            * score_scale
        ).astype(jnp.bfloat16)
        grad_buffer = lax.dynamic_update_slice_in_dim(
            grad_buffer, grad_queries, head_idx * head_dim, 2
        )
        grad_buffer = lax.dynamic_update_slice_in_dim(
            grad_buffer, grad_keys, inner_dim + head_idx * head_dim, 2
        )
        return lax.dynamic_update_slice_in_dim(
            grad_buffer, grad_values, 2 * inner_dim + head_idx * head_dim, 2
        )

    grad_qkv = lax.fori_loop(
        0,
        head_count,
        backward_head,
        jnp.zeros((window_count, window_tokens, 3 * inner_dim), jnp.bfloat16),
    )
    grad_flat = grad_qkv.reshape(-1, 3 * inner_dim)
    contract_rows = (((0,), (0,)), ((), ()))
    shard_rows = qkv_weight.shape[0]
    local_grad = lax.dot_general(
        flat_in, grad_flat, contract_rows, preferred_element_type=jnp.float32
    )
    whole_grad = lax.psum(local_grad, ("gx", "gy"))
    qkv_grad = lax.dynamic_slice_in_dim(
        whole_grad, lax.axis_index("gy") * shard_rows, shard_rows, 0
    )
    return (block_out, qkv_grad)


def solution(mesh):
    in_specs = (
        P("gx", "gy", None, None),
        P("gx", "gy", None, None),
        P(),
        P("gy", None),
        P("gy", None),
    )
    out_specs = (P("gx", "gy", None, None), P("gy", None))
    return jax.shard_map(shards, mesh=mesh, in_specs=in_specs, out_specs=out_specs, check_vma=False)
```

profile of v0, /device:TPU:0, one launch (start us, length us, event | category | flops | bytes accessed | tf_op | source)
XLA Modules:
  0.0 313.7 jit_solution(8115496946814767307)
XLA Ops:
  8.0 1.3 convert_reduce_fusion
  10.7 4.6 %collective-permute-start = (bf16[4,8,8,768]{3,2,1,0:T(8,128)(2,1)S(1)}, bf16[4,8,8,768]{3,2,1,0:T(8,128)(2,1)S(1)}, u32[]{:S(2)}, u32[]{:S(2)}) collective-permute-start(bf16[4,8,8,768]{3,2,1,0:T(8,128)(2,1)S(1)} %get-tuple-element.239), channel_id=1, source_target_pairs={{0,28},{4,0},{8,4},{12,8},{16,12},{20,16},{24,20},{28,24},{1,29},{... | collective-permute-start | bytes 1179656 | tf_op jit(solution)/shard_map/ppermute | solution.py:15
  15.3 5.3 %collective-permute-done = bf16[4,8,8,768]{3,2,1,0:T(8,128)(2,1)S(1)} collective-permute-done((bf16[4,8,8,768]{3,2,1,0:T(8,128)(2,1)S(1)}, bf16[4,8,8,768]{3,2,1,0:T(8,128)(2,1)S(1)}, u32[]{:S(2)}, u32[]{:S(2)}) %collective-permute-start) | collective-permute-done | bytes 393248 | tf_op jit(solution)/shard_map/ppermute | solution.py:15
  20.7 2.5 collective-permute-start.1
  23.2 18.8 %all_gather.7 = bf16[384,768]{1,0:T(8,128)(2,1)} all-gather(bf16[96,768]{1,0:T(8,128)(2,1)S(1)} %copy-done.3), channel_id=1, replica_groups=mesh['gx'=8,'gy'=4] {'gy'}, dimensions={0}, use_global_device_ids=true | all-gather | bytes 737280 | tf_op jit(solution)/shard_map/all_gather | solution.py:98
  42.0 13.0 %all-gather.2.cloned.1.call-done = bf16[768,1152]{1,0:T(8,128)(2,1)} async-done(((bf16[192,1152]{1,0:T(8,128)(2,1)}), bf16[768,1152]{1,0:T(8,128)(2,1)}) %all-gather.2.cloned.1.call-update) | async-done | bytes 1769488 | tf_op jit(solution)/shard_map/all_gather | solution.py:78
  55.0 2.7 fusion.43
  57.7 11.2 %while.30 = (s32[]{:T(128)}, bf16[1,512,384]{1,2,0:T(8,128)(2,1)S(1)}, bf16[1,512,1152]{2,1,0:T(8,128)(2,1)S(1)}, s32[]{:T(128)}, s32[]{:T(128)}, /*index=5*/s32...) while((s32[]{:T(128)}, bf16[1,512,384]{1,2,0:T(8,128)(2,1)S(1)}, ...), condition=%wide.region_5.6_spmd, body=%wide.region_2.5_spmd.sunk | while | flops 35404812 | bytes 3582236 | solution.py:92
  68.9 1.7 convolution_convert_fusion.3
  70.7 9.0 %collective-permute-done.2 = bf16[4,8,8,768]{3,2,1,0:T(8,128)(2,1)S(1)} collective-permute-done((bf16[4,8,8,768]{3,2,1,0:T(8,128)(2,1)S(1)}, bf16[4,8,8,768]{3,2,1,0:T(8,128)(2,1)S(1)}, u32[]{:S(2)}, u32[]{:S(2)}) %collective-permute-start.2) | collective-permute-done | bytes 393248 | tf_op jit(solution)/shard_map/ppermute | solution.py:15
  79.7 1.5 collective-permute-start.3
  81.3 7.8 %collective-permute-done.3 = bf16[8,4,8,768]{3,2,1,0:T(8,128)(2,1)S(1)} collective-permute-done((bf16[8,4,8,768]{3,2,1,0:T(8,128)(2,1)S(1)}, bf16[8,4,8,768]{3,2,1,0:T(8,128)(2,1)S(1)}, u32[]{:S(2)}, u32[]{:S(2)}) %collective-permute-start.3) | collective-permute-done | bytes 393248 | tf_op jit(solution)/shard_map/ppermute | solution.py:15
  90.3 1.5 multiply_convert_fusion.1
  92.5 5.3 %collective-permute-done.4 = bf16[4,8,8,768]{3,2,1,0:T(8,128)(2,1)S(1)} collective-permute-done((bf16[4,8,8,768]{3,2,1,0:T(8,128)(2,1)S(1)}, bf16[4,8,8,768]{3,2,1,0:T(8,128)(2,1)S(1)}, u32[]{:S(2)}, u32[]{:S(2)}) %collective-permute-start.4) | collective-permute-done | bytes 393248 | tf_op jit(solution)/shard_map/ppermute | solution.py:15
  98.5 10.7 %collective-permute-done.5 = bf16[8,4,8,768]{3,2,1,0:T(8,128)(2,1)} collective-permute-done((bf16[8,4,8,768]{3,2,1,0:T(8,128)(2,1)S(1)}, bf16[8,4,8,768]{3,2,1,0:T(8,128)(2,1)}, u32[]{:S(2)}, u32[]{:S(2)}) %collective-permute-start.5) | collective-permute-done | bytes 393248 | tf_op jit(solution)/shard_map/ppermute | solution.py:15
  109.2 1.1 pad_maximum_fusion.3
  110.9 1.1 broadcast_in_dim.25
  112.0 49.0 %while.31 = (s32[]{:T(128)}, bf16[1,512,1152]{1,2,0:T(8,128)(2,1)}, bf16[1,512,1152]{2,1,0:T(8,128)(2,1)S(1)}, bf16[1,512,384]{2,1,0:T(8,128)(2,1)S(1)}, s32[]{:...) while((s32[]{:T(128)}, bf16[1,512,1152]{1,2,0:T(8,128)(2,1)}, ...), condition=%wide.region_10.11_spmd, body=%wide.region_6.10_spmd.sunk | while | flops 88160776 | bytes 9951548 | solution.py:150
  114.2 0.9 fusion.101
  115.2 0.9 fusion.102
  118.3 0.9 fusion.101
  119.3 0.9 fusion.102
  122.4 0.9 fusion.101
  123.3 0.9 fusion.102
  126.5 0.9 fusion.101
  127.4 0.9 fusion.102
  130.5 0.9 fusion.101
  131.5 0.9 fusion.102
  133.7 0.9 fusion.100
  134.6 1.0 fusion.101
  135.6 0.9 fusion.102
  138.7 0.9 fusion.101
  139.7 0.9 fusion.102
  141.9 0.9 fusion.100
  142.8 0.9 fusion.101
  143.8 0.9 fusion.102
  146.9 0.9 fusion.101
  147.8 0.9 fusion.102
  151.0 0.9 fusion.101
  151.9 0.9 fusion.102
  155.0 0.9 fusion.101
  156.0 0.9 fusion.102
  158.2 0.9 fusion.100
  159.1 0.9 fusion.101
  160.1 0.9 fusion.102
  161.0 4.2 %fusion.50 = f32[768,1152]{1,0:T(8,128)} fusion(bf16[512,768]{1,0:T(8,128)(2,1)S(1)} %bitcast.110, bf16[1,512,1152]{1,2,0:T(8,128)(2,1)} %get-tuple-element.203), kind=kOutput, calls=%fused_computation.66 | convolution fusion | flops 905969664 | bytes 5505024 | tf_op jit(solution)/shard_map/dot_general | solution.py:159
  165.3 139.4 %all-reduce.2.cloned.1.call-done = f32[768,1152]{1,0:T(8,128)} async-done(((f32[768,1152]{1,0:T(8,128)}), f32[768,1152]{1,0:T(8,128)}) %all-reduce.2.cloned.1.call-update) | async-done | bytes 3538960 | tf_op jit(solution)/shard_map/psum | solution.py:162
  304.7 2.1 constant_dynamic-slice_fusion
  (128 shorter events, 40.3 us)
Async XLA Ops:
  7.2 2.1 copy-start
  7.2 2.5 copy-start.4
  7.2 47.9 %all-gather.2.cloned.1.call-start = ((), (), s32[]{:S(2)}) async-start(), calls=%async_computation | async-start | bytes 2211840 | tf_op jit(solution)/shard_map/all_gather | solution.py:78
  7.9 296.8 %all-reduce.2.cloned.1.call-start = ((), (), s32[]{:S(2)}) async-start(), calls=%async_computation.1 | async-start | bytes 7077888 | tf_op jit(solution)/shard_map/psum | solution.py:162
  10.7 12.5 %copy-start.3 = (bf16[96,768]{1,0:T(8,128)(2,1)S(1)}, bf16[96,768]{1,0:T(8,128)(2,1)}, u32[]{:S(2)}) copy-start(bf16[96,768]{1,0:T(8,128)(2,1)} %param.13) | copy-start | bytes 442372
  10.7 9.9 %collective-permute-start = (bf16[4,8,8,768]{3,2,1,0:T(8,128)(2,1)S(1)}, bf16[4,8,8,768]{3,2,1,0:T(8,128)(2,1)S(1)}, u32[]{:S(2)}, u32[]{:S(2)}) collective-permute-start(bf16[4,8,8,768]{3,2,1,0:T(8,128)(2,1)S(1)} %get-tuple-element.239), channel_id=1, source_target_pairs={{0,28},{4,0},{8,4},{12,8},{16,12},{20,16},{24,20},{28,24},{1,29},{... | collective-permute-start | bytes 1179656 | tf_op jit(solution)/shard_map/ppermute | solution.py:15
  20.7 21.3 %collective-permute-start.1 = (bf16[8,4,8,768]{3,2,1,0:T(8,128)(2,1)S(1)}, bf16[8,4,8,768]{3,2,1,0:T(8,128)(2,1)S(1)}, u32[]{:S(2)}, u32[]{:S(2)}) collective-permute-start(bf16[8,4,8,768]{3,2,1,0:T(8,128)(2,1)S(1)} %get-tuple-element.237), channel_id=1, source_target_pairs={{0,3},{1,0},{2,1},{3,2},{4,7},{5,4},{6,5},{7,6},{8,11},{9,8},{10,9... | collective-permute-start | bytes 1179656 | tf_op jit(solution)/shard_map/ppermute | solution.py:15
  70.7 9.1 %collective-permute-start.2 = (bf16[4,8,8,768]{3,2,1,0:T(8,128)(2,1)S(1)}, bf16[4,8,8,768]{3,2,1,0:T(8,128)(2,1)S(1)}, u32[]{:S(2)}, u32[]{:S(2)}) collective-permute-start(bf16[4,8,8,768]{3,2,1,0:T(8,128)(2,1)S(1)} %bitcast.114), channel_id=1, source_target_pairs={{0,4},{4,8},{8,12},{12,16},{16,20},{20,24},{24,28},{28,0},{1,5},{5... | collective-permute-start | bytes 1179656 | tf_op jit(solution)/shard_map/ppermute | solution.py:15
  79.7 9.3 %collective-permute-start.3 = (bf16[8,4,8,768]{3,2,1,0:T(8,128)(2,1)S(1)}, bf16[8,4,8,768]{3,2,1,0:T(8,128)(2,1)S(1)}, u32[]{:S(2)}, u32[]{:S(2)}) collective-permute-start(bf16[8,4,8,768]{3,2,1,0:T(8,128)(2,1)S(1)} %fusion.55), channel_id=1, source_target_pairs={{0,1},{1,2},{2,3},{3,0},{4,5},{5,6},{6,7},{7,4},{8,9},{9,10},{10,1... | collective-permute-start | bytes 1179656 | tf_op jit(solution)/shard_map/ppermute | solution.py:15
  89.1 1.1 copy-start.2
  92.5 5.4 %collective-permute-start.4 = (bf16[4,8,8,768]{3,2,1,0:T(8,128)(2,1)S(1)}, bf16[4,8,8,768]{3,2,1,0:T(8,128)(2,1)S(1)}, u32[]{:S(2)}, u32[]{:S(2)}) collective-permute-start(bf16[4,8,8,768]{3,2,1,0:T(8,128)(2,1)S(1)} %get-tuple-element.229), channel_id=1, source_target_pairs={{0,28},{4,0},{8,4},{12,8},{16,12},{20,16},{24,20},{28,24},{1,29},{... | collective-permute-start | bytes 1179656 | tf_op jit(solution)/shard_map/ppermute | solution.py:15
  97.9 12.4 %copy-start.1 = (bf16[384,768]{1,0:T(8,128)(2,1)S(1)}, bf16[384,768]{1,0:T(8,128)(2,1)}, u32[]{:S(2)}) copy-start(bf16[384,768]{1,0:T(8,128)(2,1)} %all_gather.7) | copy-start | bytes 1769476
  97.9 11.4 %collective-permute-start.5 = (bf16[8,4,8,768]{3,2,1,0:T(8,128)(2,1)S(1)}, bf16[8,4,8,768]{3,2,1,0:T(8,128)(2,1)}, u32[]{:S(2)}, u32[]{:S(2)}) collective-permute-start(bf16[8,4,8,768]{3,2,1,0:T(8,128)(2,1)S(1)} %get-tuple-element.227), channel_id=1, source_target_pairs={{0,3},{1,0},{2,1},{3,2},{4,7},{5,4},{6,5},{7,6},{8,11},{9,8},{10,9... | collective-permute-start | bytes 1179656 | tf_op jit(solution)/shard_map/ppermute | solution.py:15
Sparse Core Ops, SparseCore 0:
  9.8 45.1 all-gather.1
  165.4 139.2 all-reduce.1
where the time goes:
time: 314 us
  waiting for transfers between devices  191 us (61%)
  matrix products  60.9 us (19%)
  blocking collectives  18.8 us (6%)
  between operations  14.3 us (5%)
  other arithmetic  13.7 us (4%)
  starting transfers between devices  9.39 us (3%)
  local copies, waits for them, and re-layouts  5.15 us (2%)
    psum x1, waiting for transfers between devices, shards(): whole_grad = lax.psum(local_grad, ('gx', 'gy'))  139 us
    ppermute x6, waiting for transfers between devices, shifted(): lax.ppermute(x, axis, [(i, (i + by) % devices) for i in range(devices)])  38.1 us
    all_gather x1, blocking collectives, shards(): proj_whole = lax.all_gather(proj_weight, 'gy', axis=0, tiled=True)  18.8 us
    all_gather x1, waiting for transfers between devices, shards(): qkv_whole = lax.all_gather(qkv_weight, 'gy', axis=0, tiled=True)  13 us
    dot_general x12, matrix products, backward_head(): jnp.einsum('wqk,wqd->wkd', grad_scores, queries, preferred_element_type=j...  11.3 us
    dot_general x12, matrix products, backward_head(): jnp.einsum('wqk,wqd->wkd', prob_half, grad_mixed, preferred_element_type=...  11.2 us
    dot_general x12, matrix products, backward_head(): jnp.einsum('wqk,wkd->wqd', grad_scores, keys_in, preferred_element_type=j...  11 us
    dot_general x24, matrix products, head_probs(): jnp.einsum('wqd,wkd->wqk', queries, keys_in, preferred_element_type=jnp.f...  9.39 us
  transfers between devices with their start and end apart: 8, of which 7 were waited for; matrix products, arithmetic and copies ran while one was open for 1% of the time, Pallas kernels for 0%

commit v1 on v0

--- a/solution.py
+++ b/solution.py
@@ -95,7 +95,20 @@
         forward_head,
         jnp.zeros((window_count, window_tokens, inner_dim), jnp.bfloat16),
     )
-    proj_whole = lax.all_gather(proj_weight, "gy", axis=0, tiled=True)
+
+    def _register_lots_all(own_rows, a_name, dimension_no=0):
+        axis_len = lax.psum(1, axis_name=a_name)
+        d_next = sorted(((c, (c + 1) % axis_len) for c in range(axis_len)))
+        n_now = own_rows
+        blocks_here = [n_now]
+        for t in range(1, axis_len):
+            n_now = lax.ppermute(n_now, axis_name=a_name, perm=d_next)
+            blocks_here.insert(0, n_now)
+        y2 = jnp.concatenate(blocks_here, dimension_no)
+        h_now = lax.axis_index(a_name) + 1
+        return jnp.roll(y2, h_now * own_rows.shape[dimension_no], dimension_no)
+
+    proj_whole = _register_lots_all(proj_weight, "gy")
     contract_cols = (((1,), (1,)), ((), ()))
     block_shift = jnp.dot(
         attn_out.reshape(-1, inner_dim), proj_whole, preferred_element_type=jnp.float32

time: 314 us -> 287 us (0.914)
  matrix products: 60.9 us -> 37.2 us
  blocking collectives: 18.8 us -> 0 us
  waiting for transfers between devices: 191 us -> 204 us
    all_gather x1 -> x0, blocking collectives: 18.8 us -> none  [shards(): proj_whole = lax.all_gather(proj_weight, 'gy', axis=0, tiled=True)]
    ppermute x0 -> x3, waiting for transfers between devices: none -> 16.4 us  [_register_lots_all(): n_now = lax.ppermute(n_now, axis_name=a_name, perm=d_next)]
    all_gather x1, waiting for transfers between devices: 13 us -> 2.68 us  [shards(): qkv_whole = lax.all_gather(qkv_weight, 'gy', axis=0, tiled=True)]
    dot_general x12, matrix products: 11 us -> 3.62 us  [backward_head(): jnp.einsum('wqk,wkd->wqd', grad_scores, keys_in, preferred_element_type=j...]
    dot_general x12, matrix products: 11.3 us -> 3.94 us  [backward_head(): jnp.einsum('wqk,wqd->wkd', grad_scores, queries, preferred_element_type=j...]
    dot_general x12, matrix products: 11.2 us -> 4.18 us  [backward_head(): jnp.einsum('wqk,wqd->wkd', prob_half, grad_mixed, preferred_element_type=...]
    ppermute x6, waiting for transfers between devices: 38.1 us -> 44.3 us  [shifted(): lax.ppermute(x, axis, [(i, (i + by) % devices) for i in range(devices)])]
  transfers between devices with their start and end apart: 8 -> 11, of which waited for: 7 -> 10; matrix products, arithmetic and copies ran while one was open for 1% -> 1% of each run, Pallas kernels for 0% -> 0%
where the time goes in v1:
time: 287 us; the launch traced here: 286 us
  waiting for transfers between devices  204 us (71%)
  matrix products  37.2 us (13%)
  other arithmetic  14.4 us (5%)
  between operations  14.3 us (5%)
  starting transfers between devices  12.1 us (4%)
  local copies, waits for them, and re-layouts  4.21 us (1%)
    psum x1, waiting for transfers between devices, shards(): whole_grad = lax.psum(local_grad, ('gx', 'gy'))  140 us
    ppermute x6, waiting for transfers between devices, shifted(): lax.ppermute(x, axis, [(i, (i + by) % devices) for i in range(devices)])  44.3 us
    ppermute x3, waiting for transfers between devices, _register_lots_all(): n_now = lax.ppermute(n_now, axis_name=a_name, perm=d_next)  16.4 us
    dot_general x24, matrix products, head_probs(): jnp.einsum('wqd,wkd->wqk', queries, keys_in, preferred_element_type=jnp.f...  9.63 us
    ppermute x6, starting transfers between devices, shifted(): lax.ppermute(x, axis, [(i, (i + by) % devices) for i in range(devices)])  9.22 us
  transfers between devices with their start and end apart: 11, of which 10 were waited for; matrix products, arithmetic and copies ran while one was open for 1% of the time, Pallas kernels for 0%

profile of v1, /device:TPU:0, one launch (start us, length us, event | category | flops | bytes accessed | tf_op | source)
XLA Modules:
  0.0 286.4 jit_solution(820773202929017001)
XLA Ops:
  7.2 0.7 all-gather.2.cloned.1.call-update
  8.0 1.3 convert_reduce_fusion
  10.7 4.6 %collective-permute-start = (bf16[4,8,8,768]{3,2,1,0:T(8,128)(2,1)S(1)}, bf16[4,8,8,768]{3,2,1,0:T(8,128)(2,1)S(1)}, u32[]{:S(2)}, u32[]{:S(2)}) collective-permute-start(bf16[4,8,8,768]{3,2,1,0:T(8,128)(2,1)S(1)} %get-tuple-element.239), channel_id=1, source_target_pairs={{0,28},{4,0},{8,4},{12,8},{16,12},{20,16},{24,20},{28,24},{1,29},{... | collective-permute-start | bytes 1179656 | tf_op jit(solution)/shard_map/ppermute | solution.py:15
  15.3 1.5 collective-permute-start.2
  16.8 4.9 %collective-permute-done.2 = bf16[96,768]{1,0:T(8,128)(2,1)S(1)} collective-permute-done((bf16[96,768]{1,0:T(8,128)(2,1)S(1)}, bf16[96,768]{1,0:T(8,128)(2,1)S(1)}, u32[]{:S(2)}, u32[]{:S(2)}) %collective-permute-start.2) | collective-permute-done | bytes 147488 | tf_op jit(solution)/shard_map/ppermute | solution.py:105
  21.7 1.3 collective-permute-start.3
  23.0 8.5 %collective-permute-done.3 = bf16[96,768]{1,0:T(8,128)(2,1)S(1)} collective-permute-done((bf16[96,768]{1,0:T(8,128)(2,1)S(1)}, bf16[96,768]{1,0:T(8,128)(2,1)S(1)}, u32[]{:S(2)}, u32[]{:S(2)}) %collective-permute-start.3) | collective-permute-done | bytes 147488 | tf_op jit(solution)/shard_map/ppermute | solution.py:105
  31.6 3.0 %collective-permute-start.1 = (bf16[8,4,8,768]{3,2,1,0:T(8,128)(2,1)S(1)}, bf16[8,4,8,768]{3,2,1,0:T(8,128)(2,1)S(1)}, u32[]{:S(2)}, u32[]{:S(2)}) collective-permute-start(bf16[8,4,8,768]{3,2,1,0:T(8,128)(2,1)S(1)} %get-tuple-element.237), channel_id=1, source_target_pairs={{0,3},{1,0},{2,1},{3,2},{4,7},{5,4},{6,5},{7,6},{8,11},{9,8},{10,9... | collective-permute-start | bytes 1179656 | tf_op jit(solution)/shard_map/ppermute | solution.py:15
  34.6 3.0 %collective-permute-done.4 = bf16[96,768]{1,0:T(8,128)(2,1)S(1)} collective-permute-done((bf16[96,768]{1,0:T(8,128)(2,1)S(1)}, bf16[96,768]{1,0:T(8,128)(2,1)S(1)}, u32[]{:S(2)}, u32[]{:S(2)}) %collective-permute-start.4) | collective-permute-done | bytes 147488 | tf_op jit(solution)/shard_map/ppermute | solution.py:105
  37.7 10.2 %collective-permute-done.1 = bf16[8,4,8,768]{3,2,1,0:T(8,128)(2,1)S(1)} collective-permute-done((bf16[8,4,8,768]{3,2,1,0:T(8,128)(2,1)S(1)}, bf16[8,4,8,768]{3,2,1,0:T(8,128)(2,1)S(1)}, u32[]{:S(2)}, u32[]{:S(2)}) %collective-permute-start.1) | collective-permute-done | bytes 393248 | tf_op jit(solution)/shard_map/ppermute | solution.py:15
  48.0 2.7 all-gather.2.cloned.1.call-done
  50.7 2.7 fusion.43
  53.4 11.1 %while.30 = (s32[]{:T(128)}, bf16[1,512,384]{1,2,0:T(8,128)(2,1)S(1)}, bf16[1,512,1152]{2,1,0:T(8,128)(2,1)S(1)}, s32[]{:T(128)}, s32[]{:T(128)}, /*index=5*/s32...) while((s32[]{:T(128)}, bf16[1,512,384]{1,2,0:T(8,128)(2,1)S(1)}, ...), condition=%wide.region_5.6_spmd, body=%wide.region_2.5_spmd.sunk | while | flops 35404812 | bytes 3582228 | solution.py:92
  64.6 0.6 convolution_convert_fusion.3
  65.3 9.9 %collective-permute-done.5 = bf16[4,8,8,768]{3,2,1,0:T(8,128)(2,1)S(1)} collective-permute-done((bf16[4,8,8,768]{3,2,1,0:T(8,128)(2,1)S(1)}, bf16[4,8,8,768]{3,2,1,0:T(8,128)(2,1)S(1)}, u32[]{:S(2)}, u32[]{:S(2)}) %collective-permute-start.5) | collective-permute-done | bytes 393248 | tf_op jit(solution)/shard_map/ppermute | solution.py:15
  75.3 1.3 collective-permute-start.6
  76.5 8.0 %collective-permute-done.6 = bf16[8,4,8,768]{3,2,1,0:T(8,128)(2,1)S(1)} collective-permute-done((bf16[8,4,8,768]{3,2,1,0:T(8,128)(2,1)S(1)}, bf16[8,4,8,768]{3,2,1,0:T(8,128)(2,1)S(1)}, u32[]{:S(2)}, u32[]{:S(2)}) %collective-permute-start.6) | collective-permute-done | bytes 393248 | tf_op jit(solution)/shard_map/ppermute | solution.py:15
  85.0 0.8 copy-done.1
  85.8 1.5 multiply_convert_fusion.1
  88.0 5.3 %collective-permute-done.7 = bf16[4,8,8,768]{3,2,1,0:T(8,128)(2,1)S(1)} collective-permute-done((bf16[4,8,8,768]{3,2,1,0:T(8,128)(2,1)S(1)}, bf16[4,8,8,768]{3,2,1,0:T(8,128)(2,1)S(1)}, u32[]{:S(2)}, u32[]{:S(2)}) %collective-permute-start.7) | collective-permute-done | bytes 393248 | tf_op jit(solution)/shard_map/ppermute | solution.py:15
  93.3 0.8 fusion.55
  94.4 10.9 %collective-permute-done.8 = bf16[8,4,8,768]{3,2,1,0:T(8,128)(2,1)} collective-permute-done((bf16[8,4,8,768]{3,2,1,0:T(8,128)(2,1)}, bf16[8,4,8,768]{3,2,1,0:T(8,128)(2,1)}, u32[]{:S(2)}, u32[]{:S(2)}) %collective-permute-start.8) | collective-permute-done | bytes 393248 | tf_op jit(solution)/shard_map/ppermute | solution.py:15
  105.3 1.1 pad_maximum_fusion.3
  106.4 0.6 fusion.49
  107.1 27.5 %while.31 = (s32[]{:T(128)}, bf16[1,512,1152]{1,2,0:T(8,128)(2,1)S(1)}, bf16[1,512,1152]{2,1,0:T(8,128)(2,1)S(1)}, bf16[1,512,384]{2,1,0:T(8,128)(2,1)S(1)}, s32...) while((s32[]{:T(128)}, ...), condition=%wide.region_10.11_spmd, body=%wide.region_6.10_spmd.sunk | while | flops 88160776 | bytes 9951540 | solution.py:163
  107.7 0.4 multiply_reduce_fusion.2
  109.4 0.4 fusion.100
  110.0 0.4 multiply_reduce_fusion.2
  111.7 0.4 fusion.100
  112.3 0.4 multiply_reduce_fusion.2
  114.6 0.4 multiply_reduce_fusion.2
  116.2 0.4 fusion.100
  116.8 0.4 multiply_reduce_fusion.2
  118.5 0.4 fusion.100
  119.1 0.4 multiply_reduce_fusion.2
  121.4 0.4 multiply_reduce_fusion.2
  123.1 0.4 fusion.100
  123.7 0.4 multiply_reduce_fusion.2
  126.0 0.4 multiply_reduce_fusion.2
  127.7 0.4 fusion.100
  128.3 0.4 multiply_reduce_fusion.2
  130.0 0.4 fusion.100
  130.6 0.4 multiply_reduce_fusion.2
  132.2 0.4 fusion.100
  132.9 0.4 multiply_reduce_fusion.2
  134.5 3.0 %fusion.50 = f32[768,1152]{1,0:T(8,128)} fusion(bf16[512,768]{1,0:T(8,128)(2,1)S(1)} %bitcast.108, bf16[1,512,1152]{1,2,0:T(8,128)(2,1)S(1)} %get-tuple-element.203), kind=kOutput, calls=%fused_computation.66 | convolution fusion | flops 905969664 | bytes 5505024 | tf_op jit(solution)/shard_map/dot_general | solution.py:172
  137.6 139.8 %all-reduce.2.cloned.1.call-done = f32[768,1152]{1,0:T(8,128)} async-done(((f32[768,1152]{1,0:T(8,128)}), f32[768,1152]{1,0:T(8,128)}) %all-reduce.2.cloned.1.call-update) | async-done | bytes 3538960 | tf_op jit(solution)/shard_map/psum | solution.py:175
  277.4 2.1 constant_dynamic-slice_fusion
  (139 shorter events, 33.6 us)
Async XLA Ops:
  7.2 2.1 copy-start
  7.2 2.5 copy-start.3
  7.2 43.5 %all-gather.2.cloned.1.call-start = ((), (), s32[]{:S(2)}) async-start(), calls=%async_computation | async-start | bytes 2211840 | tf_op jit(solution)/shard_map/all_gather | solution.py:78
  7.9 269.5 %all-reduce.2.cloned.1.call-start = ((), (), s32[]{:S(2)}) async-start(), calls=%async_computation.1 | async-start | bytes 7077888 | tf_op jit(solution)/shard_map/psum | solution.py:175
  10.3 5.0 %copy-start.2 = (bf16[96,768]{1,0:T(8,128)(2,1)S(1)}, bf16[96,768]{1,0:T(8,128)(2,1)}, u32[]{:S(2)}) copy-start(bf16[96,768]{1,0:T(8,128)(2,1)} %param.13) | copy-start | bytes 442372
  10.7 20.8 %collective-permute-start = (bf16[4,8,8,768]{3,2,1,0:T(8,128)(2,1)S(1)}, bf16[4,8,8,768]{3,2,1,0:T(8,128)(2,1)S(1)}, u32[]{:S(2)}, u32[]{:S(2)}) collective-permute-start(bf16[4,8,8,768]{3,2,1,0:T(8,128)(2,1)S(1)} %get-tuple-element.239), channel_id=1, source_target_pairs={{0,28},{4,0},{8,4},{12,8},{16,12},{20,16},{24,20},{28,24},{1,29},{... | collective-permute-start | bytes 1179656 | tf_op jit(solution)/shard_map/ppermute | solution.py:15
  15.3 6.4 %collective-permute-start.2 = (bf16[96,768]{1,0:T(8,128)(2,1)S(1)}, bf16[96,768]{1,0:T(8,128)(2,1)S(1)}, u32[]{:S(2)}, u32[]{:S(2)}) collective-permute-start(bf16[96,768]{1,0:T(8,128)(2,1)S(1)} %copy-done.2), channel_id=1, source_target_pairs={{0,1},{1,2},{2,3},{3,0},{4,5},{5,6},{6,7},{7,4},{8,9},{9,10},{10,1... | collective-permute-start | bytes 442376 | tf_op jit(solution)/shard_map/ppermute | solution.py:105
  21.7 9.8 %collective-permute-start.3 = (bf16[96,768]{1,0:T(8,128)(2,1)S(1)}, bf16[96,768]{1,0:T(8,128)(2,1)S(1)}, u32[]{:S(2)}, u32[]{:S(2)}) collective-permute-start(bf16[96,768]{1,0:T(8,128)(2,1)S(1)} %collective-permute-done.2), channel_id=1, source_target_pairs={{0,1},{1,2},{2,3},{3,0},{4,5},{5,6},{6,7},{7,4},{8,9},{9,10},{10,1... | collective-permute-start | bytes 442376 | tf_op jit(solution)/shard_map/ppermute | solution.py:105
  31.5 6.0 %collective-permute-start.4 = (bf16[96,768]{1,0:T(8,128)(2,1)S(1)}, bf16[96,768]{1,0:T(8,128)(2,1)S(1)}, u32[]{:S(2)}, u32[]{:S(2)}) collective-permute-start(bf16[96,768]{1,0:T(8,128)(2,1)S(1)} %collective-permute-done.3), channel_id=1, source_target_pairs={{0,1},{1,2},{2,3},{3,0},{4,5},{5,6},{6,7},{7,4},{8,9},{9,10},{10,1... | collective-permute-start | bytes 442376 | tf_op jit(solution)/shard_map/ppermute | solution.py:105
  31.6 16.4 %collective-permute-start.1 = (bf16[8,4,8,768]{3,2,1,0:T(8,128)(2,1)S(1)}, bf16[8,4,8,768]{3,2,1,0:T(8,128)(2,1)S(1)}, u32[]{:S(2)}, u32[]{:S(2)}) collective-permute-start(bf16[8,4,8,768]{3,2,1,0:T(8,128)(2,1)S(1)} %get-tuple-element.237), channel_id=1, source_target_pairs={{0,3},{1,0},{2,1},{3,2},{4,7},{5,4},{6,5},{7,6},{8,11},{9,8},{10,9... | collective-permute-start | bytes 1179656 | tf_op jit(solution)/shard_map/ppermute | solution.py:15
  65.2 10.0 %collective-permute-start.5 = (bf16[4,8,8,768]{3,2,1,0:T(8,128)(2,1)S(1)}, bf16[4,8,8,768]{3,2,1,0:T(8,128)(2,1)S(1)}, u32[]{:S(2)}, u32[]{:S(2)}) collective-permute-start(bf16[4,8,8,768]{3,2,1,0:T(8,128)(2,1)S(1)} %bitcast.112), channel_id=1, source_target_pairs={{0,4},{4,8},{8,12},{12,16},{16,20},{20,24},{24,28},{28,0},{1,5},{5... | collective-permute-start | bytes 1179656 | tf_op jit(solution)/shard_map/ppermute | solution.py:15
  75.3 9.3 %collective-permute-start.6 = (bf16[8,4,8,768]{3,2,1,0:T(8,128)(2,1)S(1)}, bf16[8,4,8,768]{3,2,1,0:T(8,128)(2,1)S(1)}, u32[]{:S(2)}, u32[]{:S(2)}) collective-permute-start(bf16[8,4,8,768]{3,2,1,0:T(8,128)(2,1)S(1)} %fusion.57), channel_id=1, source_target_pairs={{0,1},{1,2},{2,3},{3,0},{4,5},{5,6},{6,7},{7,4},{8,9},{9,10},{10,1... | collective-permute-start | bytes 1179656 | tf_op jit(solution)/shard_map/ppermute | solution.py:15
  84.6 1.1 copy-start.1
  88.0 5.4 %collective-permute-start.7 = (bf16[4,8,8,768]{3,2,1,0:T(8,128)(2,1)S(1)}, bf16[4,8,8,768]{3,2,1,0:T(8,128)(2,1)S(1)}, u32[]{:S(2)}, u32[]{:S(2)}) collective-permute-start(bf16[4,8,8,768]{3,2,1,0:T(8,128)(2,1)S(1)} %get-tuple-element.229), channel_id=1, source_target_pairs={{0,28},{4,0},{8,4},{12,8},{16,12},{20,16},{24,20},{28,24},{1,29},{... | collective-permute-start | bytes 1179656 | tf_op jit(solution)/shard_map/ppermute | solution.py:15
  94.1 11.2 %collective-permute-start.8 = (bf16[8,4,8,768]{3,2,1,0:T(8,128)(2,1)}, bf16[8,4,8,768]{3,2,1,0:T(8,128)(2,1)}, u32[]{:S(2)}, u32[]{:S(2)}) collective-permute-start(bf16[8,4,8,768]{3,2,1,0:T(8,128)(2,1)} %get-tuple-element.227), channel_id=1, source_target_pairs={{0,3},{1,0},{2,1},{3,2},{4,7},{5,4},{6,5},{7,6},{8,11},{9,8},{10,9... | collective-permute-start | bytes 1179656 | tf_op jit(solution)/shard_map/ppermute | solution.py:15
Sparse Core Ops, SparseCore 0:
  9.8 40.8 all-gather.1
  137.7 139.6 all-reduce.1
